TPU v7x, 512 devices: a whole 4x4x16 slice. The times are simulated.
512 devices in a mesh: seq: 128 (over x_hi, z, y), head: 4 (over x_lo, core).
Axes of the slice: x: 4 (x_hi: 2, x_lo: 2; x = x_hi * 2 + x_lo), y: 4, z: 16, core: 2. Of those that a mesh axis runs over, the one named last changes fastest.
Arguments:
- layer_input: bfloat16 [16384, 2688], P('seq'), may hold values from -32 to 32
- grad_out: bfloat16 [16384, 2688], P('seq'), may hold values from -6 to 6
- doc_start: int32 [16384], P('seq'), may hold values from 0 to 16383, as said below
- w_query: bfloat16 [2688, 2048], P('seq', 'head'), may hold values from -0.125 to 0.125
- key_weight: bfloat16 [2688, 1024], P('seq', 'head'), may hold values from -0.125 to 0.125
- value_weight: bfloat16 [2688, 1024], P('seq', 'head'), may hold values from -0.125 to 0.125
- w_out: bfloat16 [2048, 2688], P('head', 'seq'), may hold values from -0.125 to 0.125
- q_gain: float32 [128], replicated, may hold values from 0.5 to 5, as said below
- key_norm_gain: float32 [128], replicated, may hold values from 0.5 to 5, as said below
Outputs:
- fisher_value: float32 [2688, 1024], P('seq', 'head')
- grad_input: bfloat16 [16384, 2688], P(('seq', 'head'))
Inputs may be any that keep to these rules, and one draw needn't show every extreme that they name: doc_start[t] is the first token of the document holding token t: it never falls, doc_start[t] <= t, doc_start[0] = 0, and the last token begins a document of its own. `q_gain`: positive. `key_norm_gain`: positive.
All inputs are finite; a program needn't handle non-finite values.
Results may differ from a plain program's by a relative error of at most 0.011.
Values may be sent and summed in bfloat16 or wider, within the bound.
A program may use at most 64 MiB of HBM per device.

v0:
```python
import math
import jax
import jax.numpy as jnp
from jax import lax
from jax.sharding import PartitionSpec as P

HEAD_SIZE = 128
QSCALE = 168
WINDOW = 1024
REACH = 8


def passed_along(array, axis, by):
    peers = lax.axis_size(axis)
    pairs = [(i, i + by) for i in range(peers) if 0 <= i + by < peers]
    return lax.ppermute(array, axis, pairs)


def rotary_normed(unrotated_rows, gain_vec, token_positions, head_count):
    tokens_here = unrotated_rows.shape[0]
    entries = unrotated_rows.reshape(tokens_here, head_count, HEAD_SIZE)
    mean_sq = jnp.mean(entries * entries, axis=-1, keepdims=True)
    normed = entries * lax.rsqrt(mean_sq + 1e-06) * gain_vec
    half_dim = HEAD_SIZE // 2
    frequency = jnp.exp(jnp.arange(half_dim).astype(jnp.float32) * (-math.log(10000.0) / half_dim))
    angles = token_positions.astype(jnp.float32)[:, None] * frequency[None, :]
    cosine = jnp.cos(angles)[:, None, :]
    sine_part = jnp.sin(angles)[:, None, :]
    first_half = normed[..., :half_dim]
    second_half = normed[..., half_dim:]
    return jnp.concatenate(
        [
            first_half * cosine - second_half * sine_part,
            second_half * cosine + first_half * sine_part,
        ],
        axis=-1,
    )


def attend(query_blk, key_blk, value_blk, dattn_blk, visible):
    scale = float(QSCALE) ** (-0.5)
    scores = (
        jnp.einsum("qhgd,chd->hgqc", query_blk, key_blk, preferred_element_type=jnp.float32) * scale
    )
    scores = jnp.where(visible[None, None], scores, -jnp.inf)
    top_score = jnp.max(scores, axis=-1, keepdims=True)
    expd = jnp.exp(scores - top_score)
    probs = expd / jnp.sum(expd, axis=-1, keepdims=True)
    probs_b = probs.astype(jnp.bfloat16)
    dprobs = jnp.einsum("qhgd,chd->hgqc", dattn_blk, value_blk, preferred_element_type=jnp.float32)
    delta = jnp.sum(probs * dprobs, axis=-1, keepdims=True)
    dscores = (probs * (dprobs - delta)).astype(jnp.bfloat16)
    dquery = (
        jnp.einsum("hgqc,chd->qhgd", dscores, key_blk, preferred_element_type=jnp.float32) * scale
    )
    dkey = (
        jnp.einsum("hgqc,qhgd->chd", dscores, query_blk, preferred_element_type=jnp.float32) * scale
    )
    value_grad = jnp.einsum(
        "hgqc,qhgd->chd", probs_b, dattn_blk, preferred_element_type=jnp.float32
    )
    return (dquery, dkey, value_grad)


def on_device(
    layer_input,
    grad_out,
    doc_start,
    w_query,
    key_weight,
    value_weight,
    w_out,
    q_gain,
    key_norm_gain,
):
    tok_rows = layer_input.shape[0]
    full_query, full_key, full_value = (
        lax.all_gather(w_query, "seq", axis=0, tiled=True),
        lax.all_gather(key_weight, "seq", axis=0, tiled=True),
        lax.all_gather(value_weight, "seq", axis=0, tiled=True),
    )
    query_heads = full_query.shape[1] // HEAD_SIZE
    kv_heads = full_key.shape[1] // HEAD_SIZE
    group_width = query_heads // kv_heads
    seq_index = lax.axis_index("seq")
    token_index = seq_index * tok_rows + jnp.arange(tok_rows, dtype=jnp.int32)
    token_positions = token_index - doc_start
    query_raw = jnp.dot(layer_input, full_query, preferred_element_type=jnp.float32)
    key_unrotated = jnp.dot(layer_input, full_key, preferred_element_type=jnp.float32)
    value_row_matrix = jnp.dot(layer_input, full_value, preferred_element_type=jnp.float32).astype(
        jnp.bfloat16
    )
    query_full, query_back = jax.vjp(
        lambda unrotated_rows: rotary_normed(unrotated_rows, q_gain, token_positions, query_heads),
        query_raw,
    )
    key_complete, key_backward = jax.vjp(
        lambda unrotated_rows: rotary_normed(
            unrotated_rows, key_norm_gain, token_positions, kv_heads
        ),
        key_unrotated,
    )
    query_row_matrix = query_full.astype(jnp.bfloat16)
    key_row_matrix = key_complete.astype(jnp.bfloat16)
    attention_grad = lax.dot_general(
        grad_out,
        lax.all_gather(w_out, "seq", axis=1, tiled=True),
        (((1,), (1,)), ((), ())),
        preferred_element_type=jnp.float32,
    ).astype(jnp.bfloat16)
    key_value = jnp.stack(
        [key_row_matrix.reshape(tok_rows, kv_heads * HEAD_SIZE), value_row_matrix]
    )
    earlier = [key_value]
    for distance in range(1, REACH + 1):
        earlier.append(passed_along(key_value, "seq", distance))
    context = jnp.concatenate([earlier[distance] for distance in range(REACH, -1, -1)], axis=1)
    context_len = context.shape[1]
    key_index = (seq_index - REACH) * tok_rows + jnp.arange(context_len, dtype=jnp.int32)
    visible = (
        (key_index[None, :] >= doc_start[:, None])
        & (key_index[None, :] <= token_index[:, None])
        & (token_index[:, None] - key_index[None, :] < WINDOW)
    )
    dquery, dkey, value_grad = attend(
        query_row_matrix.reshape(tok_rows, kv_heads, group_width, HEAD_SIZE),
        context[0].reshape(context_len, kv_heads, HEAD_SIZE),
        context[1].reshape(context_len, kv_heads, HEAD_SIZE),
        attention_grad.reshape(tok_rows, kv_heads, group_width, HEAD_SIZE),
        visible,
    )
    key_grads = jnp.stack(
        [
            dkey.reshape(context_len, kv_heads * HEAD_SIZE),
            value_grad.reshape(context_len, kv_heads * HEAD_SIZE),
        ]
    )

    def block_of(distance):
        first_row = (REACH - distance) * tok_rows
        return key_grads[:, first_row : first_row + tok_rows]

    owned_grads = block_of(0)
    for distance in range(1, REACH + 1):
        owned_grads = owned_grads + passed_along(block_of(distance), "seq", -distance)
    key_total = owned_grads[0].reshape(tok_rows, kv_heads, HEAD_SIZE)
    value_total = owned_grads[1]
    dquery_raw = query_back(dquery.reshape(tok_rows, query_heads, HEAD_SIZE))[0].astype(
        jnp.bfloat16
    )
    dkey_raw = key_backward(key_total)[0].astype(jnp.bfloat16)
    dvalue_rows = value_total.astype(jnp.bfloat16)
    squares = jnp.square(layer_input.astype(jnp.float32))
    value_sq = value_total * value_total
    all_tokens = lax.axis_size("seq") * tok_rows
    fisher_term = lax.dot_general(
        squares,
        value_sq,
        (((0,), (0,)), ((), ())),
        precision=lax.Precision.HIGHEST,
        preferred_element_type=jnp.float32,
    )
    fisher_value = (
        lax.psum_scatter(fisher_term, "seq", scatter_dimension=0, tiled=True) / all_tokens
    )
    contract = (((1,), (1,)), ((), ()))
    total = lax.dot_general(dquery_raw, full_query, contract, preferred_element_type=jnp.float32)
    total = total + lax.dot_general(
        dkey_raw, full_key, contract, preferred_element_type=jnp.float32
    )
    grad_input = lax.psum_scatter(
        total
        + lax.dot_general(dvalue_rows, full_value, contract, preferred_element_type=jnp.float32),
        "head",
        scatter_dimension=0,
        tiled=True,
    ).astype(jnp.bfloat16)
    return (fisher_value, grad_input)


def solution(mesh):
    in_specs = (
        P("seq", None),
        P("seq", None),
        P("seq"),
        P("seq", "head"),
        P("seq", "head"),
        P("seq", "head"),
        P("head", "seq"),
        P(),
        P(),
    )
    out_specs = (P("seq", "head"), P(("seq", "head"), None))
    return jax.shard_map(
        on_device, mesh=mesh, in_specs=in_specs, out_specs=out_specs, check_vma=False
    )
```

profile of v0, /device:TPU:32, one launch (start us, length us, event | category | flops | bytes accessed | tf_op | source)
XLA Modules:
  0.0 1421.1 jit_solution(520456489507171597)
XLA Ops:
  11.1 204.0 %all-gather.11.cloned.1.call-done = bf16[128,21,256]{2,1,0:T(8,128)(2,1)} async-done(((bf16[1,21,256]{2,1,0:T(8,128)(2,1)}), bf16[128,21,256]{2,1,0:T(8,128)(2,1)}) %all-gather.11.cloned.1.call-update) | async-done | bytes 1376272 | tf_op jit(solution)/shard_map/all_gather | solution.py:79
  215.1 2.4 reshape.224
  219.4 192.9 %all-gather.13.cloned.1.call-done = bf16[128,21,256]{2,1,0:T(8,128)(2,1)} async-done(((bf16[1,21,256]{2,1,0:T(8,128)(2,1)}), bf16[128,21,256]{2,1,0:T(8,128)(2,1)}) %all-gather.13.cloned.1.call-update) | async-done | bytes 1376272 | tf_op jit(solution)/shard_map/all_gather | solution.py:80
  412.2 2.4 reshape.226
  415.1 5.5 collective-permute-start.1
  420.6 3.4 collective-permute-start
  424.9 2.5 collective-permute-start.7
  427.4 4.8 collective-permute-start.6
  432.2 2.8 collective-permute-start.5
  435.0 5.1 collective-permute-start.2
  440.2 3.0 collective-permute-start.3
  443.2 5.7 collective-permute-start.4
  448.9 2.5 collective-permute-done.4
  452.7 1.8 copy.100
  454.5 177.1 %all-gather.15.cloned.1.call-done = bf16[128,21,512]{2,1,0:T(8,128)(2,1)} async-done(((bf16[1,21,512]{2,1,0:T(8,128)(2,1)}), bf16[128,21,512]{2,1,0:T(8,128)(2,1)}) %all-gather.15.cloned.1.call-update) | async-done | bytes 2752528 | tf_op jit(solution)/shard_map/all_gather | solution.py:107
  631.6 3.9 reshape.228
  638.3 211.3 %all-gather.9.cloned.1.call-done = bf16[128,21,512]{2,1,0:T(8,128)(2,1)} async-done(((bf16[1,21,512]{2,1,0:T(8,128)(2,1)}), bf16[128,21,512]{2,1,0:T(8,128)(2,1)}) %all-gather.9.cloned.1.call-update) | async-done | bytes 2752528 | tf_op jit(solution)/shard_map/all_gather | solution.py:78
  849.6 3.9 reshape.222
  853.5 2.4 fusion.52
  857.6 1.8 multiply_reduce_fusion.2
  864.7 3.5 fusion.51
  868.2 3.6 fusion.10
  871.8 2.5 multiply_reduce_fusion
  880.6 1.7 copy.110
  884.3 1.9 multiply_reduce_fusion.1
  887.1 3.0 fusion.26
  890.1 4.6 collective-permute-start.8
  894.7 2.9 collective-permute-start.9
  897.6 1.9 collective-permute-start.10
  900.3 1.9 collective-permute-start.11
  906.7 3.7 collective-permute-done.9
  913.0 2.1 fusion.33
  915.1 28.1 %collective-permute-done.11 = f32[2,128,256]{1,2,0:T(8,128)S(1)} collective-permute-done((f32[2,128,256]{1,2,0:T(8,128)}, f32[2,128,256]{1,2,0:T(8,128)S(1)}, u32[]{:S(2)}, u32[]{:S(2)}) %collective-permute-start.11) | collective-permute-done | bytes 262176 | tf_op jit(solution)/shard_map/ppermute | solution.py:16
  944.5 3.9 fusion.7
  960.8 369.8 %fusion = f32[24,256]{1,0:T(8,128)S(1)} fusion(f32[2688,256]{1,0:T(8,128)S(1)} %copy-done.7), kind=kCustom, calls=%all-reduce-scatter | all-reduce-scatter fusion | flops 786433 | bytes 2779136
  1334.5 22.1 %collective-permute-start.28 = (f32[24,256]{1,0:T(8,128)S(1)}, f32[24,256]{1,0:T(8,128)S(1)}, u32[]{:S(2)}, u32[]{:S(2)}) collective-permute-start(f32[24,256]{1,0:T(8,128)S(1)} %fusion), channel_id=1, source_target_pairs={{0,52},{4,56},{8,60},{12,64},{16,68},{20,72},{24,76},{28,80},{32,8... | collective-permute-start | bytes 73736
  1358.0 1.8 collective-permute-start.26
  1359.8 12.5 collective-permute-start.25
  1372.3 1.9 collective-permute-start.24
  1374.2 2.5 collective-permute-start.23
  1376.8 3.1 collective-permute-start.22
  1379.9 4.9 collective-permute-start.21
  1386.1 8.2 collective-permute-start.19
  1394.3 3.7 collective-permute-start.18
  1398.1 4.2 collective-permute-start.17
  1402.3 1.9 collective-permute-start.16
  1406.2 3.9 collective-permute-done.16
  1410.2 2.1 concatenate.21
  (168 shorter events, 58.4 us)
Async XLA Ops:
  7.2 628.3 %copy-start = (bf16[128,2688]{1,0:T(8,128)(2,1)S(1)}, bf16[128,2688]{1,0:T(8,128)(2,1)}, u32[]{:S(2)}) copy-start(bf16[128,2688]{1,0:T(8,128)(2,1)} %param.10) | copy-start | bytes 2064388
  7.2 207.9 %all-gather.11.cloned.1.call-start = ((), (), s32[]{:S(2)}) async-start(), calls=%async_computation.3 | async-start | bytes 1585152 | tf_op jit(solution)/shard_map/all_gather | solution.py:79
  7.9 404.3 %all-gather.13.cloned.1.call-start = ((), (), s32[]{:S(2)}) async-start(), calls=%async_computation.4 | async-start | bytes 1585152 | tf_op jit(solution)/shard_map/all_gather | solution.py:80
  8.7 622.9 %all-gather.15.cloned.1.call-start = ((), (), s32[]{:S(2)}) async-start(), calls=%async_computation.5 | async-start | bytes 3170304 | tf_op jit(solution)/shard_map/all_gather | solution.py:107
  9.4 840.3 %all-gather.9.cloned.1.call-start = ((), (), s32[]{:S(2)}) async-start(), calls=%async_computation.2 | async-start | bytes 3170304 | tf_op jit(solution)/shard_map/all_gather | solution.py:78
  10.0 1402.9 %reduce-scatter.4.cloned.1.call-start = ((), (), s32[]{:S(2)}) async-start(), calls=%async_computation.1 | async-start | bytes 1720320 | tf_op jit(solution)/shard_map/reduce_scatter | solution.py:171
  11.0 207.8 %copy-start.18 = (f32[128,64]{1,0:T(8,128)}, f32[128,64]{1,0:T(8,128)S(1)}, u32[]{:S(2)}) copy-start(f32[128,64]{1,0:T(8,128)S(1)} %get-tuple-element.25) | copy-start | bytes 98308
  11.0 206.4 %copy-start.5 = (bf16[128,2688]{1,0:T(8,128)(2,1)S(1)}, bf16[128,2688]{1,0:T(8,128)(2,1)}, u32[]{:S(2)}) copy-start(bf16[128,2688]{1,0:T(8,128)(2,1)} %param.9) | copy-start | bytes 2064388
  217.9 196.7 %copy-start.11 = (f32[128,2,128]{2,1,0:T(2,128)}, f32[128,2,128]{2,1,0:T(2,128)S(1)}, u32[]{:S(2)}) copy-start(f32[128,2,128]{2,1,0:T(2,128)S(1)} %reshape.218) | copy-start | bytes 393220
  218.6 196.0 %copy-start.21 = (f32[128,2]{1,0:T(8,128)}, f32[128,2]{1,0:T(8,128)S(1)}, u32[]{:S(2)}) copy-start(f32[128,2]{1,0:T(8,128)S(1)} %copy.76) | copy-start | bytes 3076
  414.7 25.5 %copy-start.3 = (bf16[2688,256]{1,0:T(8,128)(2,1)}, bf16[2688,256]{1,0:T(8,128)(2,1)S(1)}, u32[]{:S(2)}) copy-start(bf16[2688,256]{1,0:T(8,128)(2,1)S(1)} %reshape.226) | copy-start | bytes 4128772
  414.7 9.3 copy-start.26
  415.1 25.1 %collective-permute-start.1 = (bf16[2,128,256]{2,1,0:T(8,128)(2,1)S(1)}, bf16[2,128,256]{2,1,0:T(8,128)(2,1)S(1)}, u32[]{:S(2)}, u32[]{:S(2)}) collective-permute-start(bf16[2,128,256]{2,1,0:T(8,128)(2,1)S(1)} %pad_maximum_fusion.2), channel_id=1, source_target_pairs={{0,28},{4,32},{8,36},{12,40},{16,44},{20,48},{24,52},{28,56},{32,6... | collective-permute-start | bytes 393224 | tf_op jit(solution)/shard_map/ppermute | solution.py:16
  420.6 14.4 %collective-permute-start = (bf16[2,128,256]{2,1,0:T(8,128)(2,1)S(1)}, bf16[2,128,256]{2,1,0:T(8,128)(2,1)S(1)}, u32[]{:S(2)}, u32[]{:S(2)}) collective-permute-start(bf16[2,128,256]{2,1,0:T(8,128)(2,1)S(1)} %pad_maximum_fusion.2), channel_id=1, source_target_pairs={{0,32},{4,36},{8,40},{12,44},{16,48},{20,52},{24,56},{28,60},{32,6... | collective-permute-start | bytes 393224 | tf_op jit(solution)/shard_map/ppermute | solution.py:16
  424.9 26.6 %collective-permute-start.7 = (bf16[2,128,256]{2,1,0:T(8,128)(2,1)S(1)}, bf16[2,128,256]{2,1,0:T(8,128)(2,1)S(1)}, u32[]{:S(2)}, u32[]{:S(2)}) collective-permute-start(bf16[2,128,256]{2,1,0:T(8,128)(2,1)S(1)} %pad_maximum_fusion.2), channel_id=1, source_target_pairs={{0,4},{4,8},{8,12},{12,16},{16,20},{20,24},{24,28},{28,32},{32,36}... | collective-permute-start | bytes 393224 | tf_op jit(solution)/shard_map/ppermute | solution.py:16
  427.4 24.1 %collective-permute-start.6 = (bf16[2,128,256]{2,1,0:T(8,128)(2,1)S(1)}, bf16[2,128,256]{2,1,0:T(8,128)(2,1)S(1)}, u32[]{:S(2)}, u32[]{:S(2)}) collective-permute-start(bf16[2,128,256]{2,1,0:T(8,128)(2,1)S(1)} %pad_maximum_fusion.2), channel_id=1, source_target_pairs={{0,8},{4,12},{8,16},{12,20},{16,24},{20,28},{24,32},{28,36},{32,40... | collective-permute-start | bytes 393224 | tf_op jit(solution)/shard_map/ppermute | solution.py:16
  432.2 19.2 %collective-permute-start.5 = (bf16[2,128,256]{2,1,0:T(8,128)(2,1)S(1)}, bf16[2,128,256]{2,1,0:T(8,128)(2,1)S(1)}, u32[]{:S(2)}, u32[]{:S(2)}) collective-permute-start(bf16[2,128,256]{2,1,0:T(8,128)(2,1)S(1)} %pad_maximum_fusion.2), channel_id=1, source_target_pairs={{0,12},{4,16},{8,20},{12,24},{16,28},{20,32},{24,36},{28,40},{32,4... | collective-permute-start | bytes 393224 | tf_op jit(solution)/shard_map/ppermute | solution.py:16
  435.0 8.1 collective-permute-start.2
  440.2 8.8 collective-permute-start.3
  443.2 8.2 collective-permute-start.4
  890.1 15.2 %collective-permute-start.8 = (f32[2,128,256]{1,2,0:T(8,128)}, f32[2,128,256]{1,2,0:T(8,128)}, u32[]{:S(2)}, u32[]{:S(2)}) collective-permute-start(f32[2,128,256]{1,2,0:T(8,128)} %get-tuple-element.2), channel_id=1, source_target_pairs={{4,0},{8,4},{12,8},{16,12},{20,16},{24,20},{28,24},{32,28},{36,32}... | collective-permute-start | bytes 786440 | tf_op jit(solution)/shard_map/ppermute | solution.py:16
  894.7 15.6 %collective-permute-start.9 = (f32[2,128,256]{1,2,0:T(8,128)}, f32[2,128,256]{1,2,0:T(8,128)}, u32[]{:S(2)}, u32[]{:S(2)}) collective-permute-start(f32[2,128,256]{1,2,0:T(8,128)} %get-tuple-element.3), channel_id=1, source_target_pairs={{8,0},{12,4},{16,8},{20,12},{24,16},{28,20},{32,24},{36,28},{40,32... | collective-permute-start | bytes 786440 | tf_op jit(solution)/shard_map/ppermute | solution.py:16
  897.6 14.0 collective-permute-start.10
  900.3 42.8 %collective-permute-start.11 = (f32[2,128,256]{1,2,0:T(8,128)}, f32[2,128,256]{1,2,0:T(8,128)S(1)}, u32[]{:S(2)}, u32[]{:S(2)}) collective-permute-start(f32[2,128,256]{1,2,0:T(8,128)} %get-tuple-element.5), channel_id=1, source_target_pairs={{16,0},{20,4},{24,8},{28,12},{32,16},{36,20},{40,24},{44,28},{48,3... | collective-permute-start | bytes 786440 | tf_op jit(solution)/shard_map/ppermute | solution.py:16
  902.2 40.9 %collective-permute-start.12 = (f32[2,128,256]{1,2,0:T(8,128)}, f32[2,128,256]{1,2,0:T(8,128)S(1)}, u32[]{:S(2)}, u32[]{:S(2)}) collective-permute-start(f32[2,128,256]{1,2,0:T(8,128)} %get-tuple-element.6), channel_id=1, source_target_pairs={{20,0},{24,4},{28,8},{32,12},{36,16},{40,20},{44,24},{48,28},{52,3... | collective-permute-start | bytes 786440 | tf_op jit(solution)/shard_map/ppermute | solution.py:16
  905.4 37.8 %collective-permute-start.13 = (f32[2,128,256]{1,2,0:T(8,128)}, f32[2,128,256]{1,2,0:T(8,128)S(1)}, u32[]{:S(2)}, u32[]{:S(2)}) collective-permute-start(f32[2,128,256]{1,2,0:T(8,128)} %get-tuple-element.7), channel_id=1, source_target_pairs={{24,0},{28,4},{32,8},{36,12},{40,16},{44,20},{48,24},{52,28},{56,3... | collective-permute-start | bytes 786440 | tf_op jit(solution)/shard_map/ppermute | solution.py:16
  910.3 32.8 %collective-permute-start.15 = (f32[2,128,256]{1,2,0:T(8,128)}, f32[2,128,256]{1,2,0:T(8,128)S(1)}, u32[]{:S(2)}, u32[]{:S(2)}) collective-permute-start(f32[2,128,256]{1,2,0:T(8,128)} %get-tuple-element.8), channel_id=1, source_target_pairs={{32,0},{36,4},{40,8},{44,12},{48,16},{52,20},{56,24},{60,28},{64,3... | collective-permute-start | bytes 786440 | tf_op jit(solution)/shard_map/ppermute | solution.py:16
  911.6 31.5 %collective-permute-start.14 = (f32[2,128,256]{1,2,0:T(8,128)}, f32[2,128,256]{1,2,0:T(8,128)S(1)}, u32[]{:S(2)}, u32[]{:S(2)}) collective-permute-start(f32[2,128,256]{1,2,0:T(8,128)} %get-tuple-element.9), channel_id=1, source_target_pairs={{28,0},{32,4},{36,8},{40,12},{44,16},{48,20},{52,24},{56,28},{60,3... | collective-permute-start | bytes 786440 | tf_op jit(solution)/shard_map/ppermute | solution.py:16
  912.9 30.2 %copy-start.8 = (f32[2,128,1152]{2,1,0:T(8,128)S(1)}, f32[2,128,1152]{2,1,0:T(8,128)}, u32[]{:S(2)}) copy-start(f32[2,128,1152]{2,1,0:T(8,128)} %fusion.6) | copy-start | bytes 3538948
  913.0 30.2 %copy-start.10 = (f32[2,128,1152,1]{2,1,3,0:T(8,128)S(1)}, f32[2,128,1152,1]{2,1,3,0:T(8,128)}, u32[]{:S(2)}) copy-start(f32[2,128,1152,1]{2,1,3,0:T(8,128)} %fusion.10) | copy-start | bytes 3538948
  915.1 29.4 %copy-start.6 = (bf16[128,2688]{1,0:T(8,128)(2,1)S(1)}, bf16[128,2688]{1,0:T(8,128)(2,1)}, u32[]{:S(2)}) copy-start(bf16[128,2688]{1,0:T(8,128)(2,1)} %param.9) | copy-start | bytes 2064388
  944.5 12.6 copy-start.9
  1330.6 27.3 %collective-permute-start.31 = (f32[21,256]{1,0:T(8,128)S(1)}, f32[21,256]{1,0:T(8,128)S(1)}, u32[]{:S(2)}, u32[]{:S(2)}) collective-permute-start(f32[21,256]{1,0:T(8,128)S(1)} %slice.92), channel_id=1, source_target_pairs={{0,64},{4,68},{8,72},{12,76},{16,80},{20,84},{24,88},{28,92},{32,9... | collective-permute-start | bytes 64520
  1331.9 27.9 %collective-permute-start.30 = (f32[24,256]{1,0:T(8,128)S(1)}, f32[24,256]{1,0:T(8,128)S(1)}, u32[]{:S(2)}, u32[]{:S(2)}) collective-permute-start(f32[24,256]{1,0:T(8,128)S(1)} %fusion), channel_id=1, source_target_pairs={{0,60},{4,64},{8,68},{12,72},{16,76},{20,80},{24,84},{28,88},{32,9... | collective-permute-start | bytes 73736
  1333.2 39.1 %collective-permute-start.29 = (f32[24,256]{1,0:T(8,128)S(1)}, f32[24,256]{1,0:T(8,128)S(1)}, u32[]{:S(2)}, u32[]{:S(2)}) collective-permute-start(f32[24,256]{1,0:T(8,128)S(1)} %fusion), channel_id=1, source_target_pairs={{0,56},{4,60},{8,64},{12,68},{16,72},{20,76},{24,80},{28,84},{32,8... | collective-permute-start | bytes 73736
  1334.5 39.7 %collective-permute-start.28 = (f32[24,256]{1,0:T(8,128)S(1)}, f32[24,256]{1,0:T(8,128)S(1)}, u32[]{:S(2)}, u32[]{:S(2)}) collective-permute-start(f32[24,256]{1,0:T(8,128)S(1)} %fusion), channel_id=1, source_target_pairs={{0,52},{4,56},{8,60},{12,64},{16,68},{20,72},{24,76},{28,80},{32,8... | collective-permute-start | bytes 73736
  1356.6 20.1 %collective-permute-start.27 = (f32[24,256]{1,0:T(8,128)S(1)}, f32[24,256]{1,0:T(8,128)S(1)}, u32[]{:S(2)}, u32[]{:S(2)}) collective-permute-start(f32[24,256]{1,0:T(8,128)S(1)} %fusion), channel_id=1, source_target_pairs={{0,48},{4,52},{8,56},{12,60},{16,64},{20,68},{24,72},{28,76},{32,8... | collective-permute-start | bytes 73736
  1358.0 21.9 %collective-permute-start.26 = (f32[24,256]{1,0:T(8,128)S(1)}, f32[24,256]{1,0:T(8,128)S(1)}, u32[]{:S(2)}, u32[]{:S(2)}) collective-permute-start(f32[24,256]{1,0:T(8,128)S(1)} %fusion), channel_id=1, source_target_pairs={{0,44},{4,48},{8,52},{12,56},{16,60},{20,64},{24,68},{28,72},{32,7... | collective-permute-start | bytes 73736
  1359.8 25.0 %collective-permute-start.25 = (f32[24,256]{1,0:T(8,128)S(1)}, f32[24,256]{1,0:T(8,128)S(1)}, u32[]{:S(2)}, u32[]{:S(2)}) collective-permute-start(f32[24,256]{1,0:T(8,128)S(1)} %fusion), channel_id=1, source_target_pairs={{0,40},{4,44},{8,48},{12,52},{16,56},{20,60},{24,64},{28,68},{32,7... | collective-permute-start | bytes 73736
  1372.3 13.8 collective-permute-start.24
  1374.2 20.1 %collective-permute-start.23 = (f32[24,256]{1,0:T(8,128)S(1)}, f32[24,256]{1,0:T(8,128)S(1)}, u32[]{:S(2)}, u32[]{:S(2)}) collective-permute-start(f32[24,256]{1,0:T(8,128)S(1)} %fusion), channel_id=1, source_target_pairs={{0,32},{4,36},{8,40},{12,44},{16,48},{20,52},{24,56},{28,60},{32,6... | collective-permute-start | bytes 73736
  1376.8 21.3 %collective-permute-start.22 = (f32[24,256]{1,0:T(8,128)S(1)}, f32[24,256]{1,0:T(8,128)S(1)}, u32[]{:S(2)}, u32[]{:S(2)}) collective-permute-start(f32[24,256]{1,0:T(8,128)S(1)} %fusion), channel_id=1, source_target_pairs={{0,28},{4,32},{8,36},{12,40},{16,44},{20,48},{24,52},{28,56},{32,6... | collective-permute-start | bytes 73736
  1379.9 22.5 %collective-permute-start.21 = (f32[24,256]{1,0:T(8,128)S(1)}, f32[24,256]{1,0:T(8,128)S(1)}, u32[]{:S(2)}, u32[]{:S(2)}) collective-permute-start(f32[24,256]{1,0:T(8,128)S(1)} %fusion), channel_id=1, source_target_pairs={{0,24},{4,28},{8,32},{12,36},{16,40},{20,44},{24,48},{28,52},{32,5... | collective-permute-start | bytes 73736
  1384.8 21.4 %collective-permute-start.20 = (f32[24,256]{1,0:T(8,128)S(1)}, f32[24,256]{1,0:T(8,128)S(1)}, u32[]{:S(2)}, u32[]{:S(2)}) collective-permute-start(f32[24,256]{1,0:T(8,128)S(1)} %fusion), channel_id=1, source_target_pairs={{0,20},{4,24},{8,28},{12,32},{16,36},{20,40},{24,44},{28,48},{32,5... | collective-permute-start | bytes 73736
  1386.1 20.1 %collective-permute-start.19 = (f32[24,256]{1,0:T(8,128)S(1)}, f32[24,256]{1,0:T(8,128)S(1)}, u32[]{:S(2)}, u32[]{:S(2)}) collective-permute-start(f32[24,256]{1,0:T(8,128)S(1)} %fusion), channel_id=1, source_target_pairs={{0,16},{4,20},{8,24},{12,28},{16,32},{20,36},{24,40},{28,44},{32,4... | collective-permute-start | bytes 73736
  1394.3 11.9 collective-permute-start.18
  1398.1 8.1 collective-permute-start.17
  1402.3 7.8 collective-permute-start.16
  (16 other events, 35.8 us)
Sparse Core Ops, SparseCore 0:
  12.3 202.7 all-gather.10
  219.3 192.8 all-gather.12
  416.8 214.6 all-gather.14
  636.0 213.6 all-gather.8
  960.3 36.5 reduce-scatter.3
where the time goes:
time: 1420 us
  waiting for transfers between devices  826 us (58%)
  blocking collectives  370 us (26%)
  starting transfers between devices  123 us (9%)
  local copies, waits for them, and re-layouts  40 us (3%)
  matrix products  24.2 us (2%)
  other arithmetic  22.4 us (2%)
  between operations  15.5 us (1%)
    unnamed x1, blocking collectives  370 us
    all_gather x1, waiting for transfers between devices, on_device(): lax.all_gather(w_query, 'seq', axis=0, tiled=True)  211 us
    all_gather x1, waiting for transfers between devices, on_device(): lax.all_gather(key_weight, 'seq', axis=0, tiled=True)  204 us
    all_gather x1, waiting for transfers between devices, on_device(): lax.all_gather(value_weight, 'seq', axis=0, tiled=True)  193 us
    all_gather x1, waiting for transfers between devices, on_device(): lax.all_gather(w_out, 'seq', axis=1, tiled=True)  177 us
    unnamed x16, starting transfers between devices  73.4 us
    ppermute x16, starting transfers between devices, passed_along(): return lax.ppermute(array, axis, pairs)  49.4 us
    ppermute x16, waiting for transfers between devices, passed_along(): return lax.ppermute(array, axis, pairs)  34.2 us
  transfers between devices with their start and end apart: 37, of which 8 were waited for; matrix products, arithmetic and copies ran while one was open for 28% of the time, Pallas kernels for 0%

commit v1 on v0

--- a/solution.py
+++ b/solution.py
@@ -104,7 +104,9 @@
     key_row_matrix = key_complete.astype(jnp.bfloat16)
     attention_grad = lax.dot_general(
         grad_out,
-        lax.all_gather(w_out, "seq", axis=1, tiled=True),
+        jnp.concatenate(
+            lax.all_to_all(jnp.stack([w_out] * lax.axis_size("seq")), "seq", 0, 0), axis=1
+        ),
         (((1,), (1,)), ((), ())),
         preferred_element_type=jnp.float32,
     ).astype(jnp.bfloat16)

time: 1420 us -> 1230 us (0.87)
  waiting for transfers between devices: 826 us -> 601 us
  starting transfers between devices: 123 us -> 160 us
    all_gather x1 -> x0, waiting for transfers between devices: 177 us -> none  [on_device(): lax.all_gather(w_out, 'seq', axis=1, tiled=True)]
    all_gather x1, waiting for transfers between devices: 211 us -> 176 us  [on_device(): lax.all_gather(w_query, 'seq', axis=0, tiled=True)]
    all_to_all x0 -> x1, starting transfers between devices: none -> 22.2 us  [on_device(): lax.all_to_all(jnp.stack([w_out] * lax.axis_size('seq')), 'seq', 0, 0)]
    ppermute x16, waiting for transfers between devices: 34.2 us -> 14.1 us  [passed_along(): return lax.ppermute(array, axis, pairs)]
  transfers between devices with their start and end apart: 37 -> 37, of which waited for: 8 -> 8; matrix products, arithmetic and copies ran while one was open for 28% -> 33% of each run, Pallas kernels for 0% -> 0%
where the time goes in v1:
time: 1230 us
  waiting for transfers between devices  601 us (49%)
  blocking collectives  362 us (29%)
  starting transfers between devices  160 us (13%)
  local copies, waits for them, and re-layouts  45.5 us (4%)
  matrix products  25 us (2%)
  other arithmetic  20.3 us (2%)
  between operations  15.4 us (1%)
    unnamed x1, blocking collectives  362 us
    all_gather x1, waiting for transfers between devices, on_device(): lax.all_gather(key_weight, 'seq', axis=0, tiled=True)  212 us
    all_gather x1, waiting for transfers between devices, on_device(): lax.all_gather(value_weight, 'seq', axis=0, tiled=True)  193 us
    all_gather x1, waiting for transfers between devices, on_device(): lax.all_gather(w_query, 'seq', axis=0, tiled=True)  176 us
    unnamed x16, starting transfers between devices  78.3 us
    ppermute x16, starting transfers between devices, passed_along(): return lax.ppermute(array, axis, pairs)  59.8 us
    unnamed x76, local copies, waits for them, and re-layouts  24.6 us
  transfers between devices with their start and end apart: 37, of which 8 were waited for; matrix products, arithmetic and copies ran while one was open for 33% of the time, Pallas kernels for 0%

profile of v1, /device:TPU:32, one launch (start us, length us, event | category | flops | bytes accessed | tf_op | source)
XLA Modules:
  0.0 1229.7 jit_solution(1825517257365681963)
XLA Ops:
  7.9 2.6 stack.10
  10.5 22.2 %all-to-all-start = ((bf16[128,512,21]{1,2,0:T(8,128)(2,1)}), bf16[128,512,21]{1,2,0:T(8,128)(2,1)}, u32[]{:S(2)}, u32[]{:S(2)}) async-start(bf16[128,512,21]{1,2,0:T(8,128)(2,1)} %stack.10), calls=%async_computation | async-start | bytes 6291456 | tf_op jit(solution)/shard_map/all_to_all | solution.py:108
  34.6 212.4 %all-gather.9.cloned.1.call-done = bf16[128,21,256]{2,1,0:T(8,128)(2,1)} async-done(((bf16[1,21,256]{2,1,0:T(8,128)(2,1)}), bf16[128,21,256]{2,1,0:T(8,128)(2,1)}) %all-gather.9.cloned.1.call-update) | async-done | bytes 1376272 | tf_op jit(solution)/shard_map/all_gather | solution.py:79
  247.0 2.4 reshape.234
  251.3 192.9 %all-gather.11.cloned.1.call-done = bf16[128,21,256]{2,1,0:T(8,128)(2,1)} async-done(((bf16[1,21,256]{2,1,0:T(8,128)(2,1)}), bf16[128,21,256]{2,1,0:T(8,128)(2,1)}) %all-gather.11.cloned.1.call-update) | async-done | bytes 1376272 | tf_op jit(solution)/shard_map/all_gather | solution.py:80
  444.2 2.4 reshape.236
  447.0 4.5 collective-permute-start
  451.5 4.4 collective-permute-start.1
  456.8 4.1 collective-permute-start.2
  460.9 2.8 collective-permute-start.3
  463.8 4.4 collective-permute-start.4
  468.2 3.9 collective-permute-start.5
  472.2 3.3 collective-permute-start.6
  475.6 2.2 collective-permute-start.7
  477.9 3.7 collective-permute-done.6
  481.5 3.1 collective-permute-done.7
  487.6 175.7 %all-gather.7.cloned.1.call-done = bf16[128,21,512]{2,1,0:T(8,128)(2,1)} async-done(((bf16[1,21,512]{2,1,0:T(8,128)(2,1)}), bf16[128,21,512]{2,1,0:T(8,128)(2,1)}) %all-gather.7.cloned.1.call-update) | async-done | bytes 2752528 | tf_op jit(solution)/shard_map/all_gather | solution.py:78
  663.3 3.9 reshape.232
  667.2 2.4 fusion.52
  671.3 1.8 multiply_reduce_fusion.2
  678.3 3.6 fusion.51
  681.9 5.4 reshape.228
  687.3 3.0 convolution_convert_fusion
  691.9 3.6 fusion.10
  695.6 2.5 multiply_reduce_fusion
  708.4 2.4 collective-permute-start.11
  717.0 1.9 multiply_reduce_fusion.1
  722.3 3.5 collective-permute-start.10
  725.8 9.3 collective-permute-start.9
  735.2 9.7 collective-permute-start.8
  744.9 2.1 fusion.33
  747.0 7.3 collective-permute-done.11
  755.9 3.9 fusion.7
  760.4 1.8 copy.113
  772.3 362.0 %fusion = f32[24,256]{1,0:T(8,128)S(1)} fusion(f32[2688,256]{1,0:T(8,128)S(1)} %copy-done.7), kind=kCustom, calls=%all-reduce-scatter | all-reduce-scatter fusion | flops 786433 | bytes 2779136
  1138.3 31.5 %collective-permute-start.28 = (f32[24,256]{1,0:T(8,128)S(1)}, f32[24,256]{1,0:T(8,128)S(1)}, u32[]{:S(2)}, u32[]{:S(2)}) collective-permute-start(f32[24,256]{1,0:T(8,128)S(1)} %fusion), channel_id=1, source_target_pairs={{0,52},{4,56},{8,60},{12,64},{16,68},{20,72},{24,76},{28,80},{32,8... | collective-permute-start | bytes 73736
  1172.4 16.1 %collective-permute-start.25 = (f32[24,256]{1,0:T(8,128)S(1)}, f32[24,256]{1,0:T(8,128)S(1)}, u32[]{:S(2)}, u32[]{:S(2)}) collective-permute-start(f32[24,256]{1,0:T(8,128)S(1)} %fusion), channel_id=1, source_target_pairs={{0,40},{4,44},{8,48},{12,52},{16,56},{20,60},{24,64},{28,68},{32,7... | collective-permute-start | bytes 73736
  1188.5 1.9 collective-permute-start.24
  1190.4 2.5 collective-permute-start.23
  1193.0 3.1 collective-permute-start.22
  1196.0 2.2 collective-permute-start.21
  1198.3 2.5 collective-permute-start.20
  1200.8 4.2 collective-permute-start.19
  1205.1 2.0 collective-permute-start.18
  1207.0 3.9 collective-permute-start.17
  1211.0 1.9 collective-permute-start.16
  1215.1 3.7 collective-permute-done.16
  1218.8 2.1 concatenate.21
  (172 shorter events, 59.6 us)
Async XLA Ops:
  7.2 680.1 %copy-start = (bf16[128,2688]{1,0:T(8,128)(2,1)S(1)}, bf16[128,2688]{1,0:T(8,128)(2,1)}, u32[]{:S(2)}) copy-start(bf16[128,2688]{1,0:T(8,128)(2,1)} %param.10) | copy-start | bytes 2064388
  7.2 239.9 %all-gather.9.cloned.1.call-start = ((), (), s32[]{:S(2)}) async-start(), calls=%async_computation.4 | async-start | bytes 1585152 | tf_op jit(solution)/shard_map/all_gather | solution.py:79
  10.5 23.7 %copy-start.28 = (s32[128]{0:T(128)S(1)}, s32[128]{0:T(128)}, u32[]{:S(2)}) copy-start(s32[128]{0:T(128)} %param.11) | copy-start | bytes 1540
  10.5 671.4 %all-to-all-start = ((bf16[128,512,21]{1,2,0:T(8,128)(2,1)}), bf16[128,512,21]{1,2,0:T(8,128)(2,1)}, u32[]{:S(2)}, u32[]{:S(2)}) async-start(bf16[128,512,21]{1,2,0:T(8,128)(2,1)} %stack.10), calls=%async_computation | async-start | bytes 6291456 | tf_op jit(solution)/shard_map/all_to_all | solution.py:108
  32.7 411.5 %all-gather.11.cloned.1.call-start = ((), (), s32[]{:S(2)}) async-start(), calls=%async_computation.5 | async-start | bytes 1585152 | tf_op jit(solution)/shard_map/all_gather | solution.py:80
  33.4 629.9 %all-gather.7.cloned.1.call-start = ((), (), s32[]{:S(2)}) async-start(), calls=%async_computation.3 | async-start | bytes 3170304 | tf_op jit(solution)/shard_map/all_gather | solution.py:78
  34.2 1187.4 %reduce-scatter.4.cloned.1.call-start = ((), (), s32[]{:S(2)}) async-start(), calls=%async_computation.2 | async-start | bytes 1720320 | tf_op jit(solution)/shard_map/reduce_scatter | solution.py:173
  34.6 216.2 %copy-start.20 = (f32[128,64]{1,0:T(8,128)}, f32[128,64]{1,0:T(8,128)S(1)}, u32[]{:S(2)}) copy-start(f32[128,64]{1,0:T(8,128)S(1)} %get-tuple-element.25) | copy-start | bytes 98308
  34.6 214.8 %copy-start.5 = (bf16[128,2688]{1,0:T(8,128)(2,1)S(1)}, bf16[128,2688]{1,0:T(8,128)(2,1)}, u32[]{:S(2)}) copy-start(bf16[128,2688]{1,0:T(8,128)(2,1)} %param.9) | copy-start | bytes 2064388
  249.9 196.7 %copy-start.13 = (f32[128,2,128]{2,1,0:T(2,128)}, f32[128,2,128]{2,1,0:T(2,128)S(1)}, u32[]{:S(2)}) copy-start(f32[128,2,128]{2,1,0:T(2,128)S(1)} %reshape.226) | copy-start | bytes 393220
  250.6 196.0 %copy-start.23 = (f32[128,2]{1,0:T(8,128)}, f32[128,2]{1,0:T(8,128)S(1)}, u32[]{:S(2)}) copy-start(f32[128,2]{1,0:T(8,128)S(1)} %copy.77) | copy-start | bytes 3076
  446.6 25.5 %copy-start.3 = (bf16[2688,256]{1,0:T(8,128)(2,1)}, bf16[2688,256]{1,0:T(8,128)(2,1)S(1)}, u32[]{:S(2)}) copy-start(bf16[2688,256]{1,0:T(8,128)(2,1)S(1)} %reshape.236) | copy-start | bytes 4128772
  447.0 21.2 %collective-permute-start = (bf16[2,128,256]{2,1,0:T(8,128)(2,1)S(1)}, bf16[2,128,256]{2,1,0:T(8,128)(2,1)S(1)}, u32[]{:S(2)}, u32[]{:S(2)}) collective-permute-start(bf16[2,128,256]{2,1,0:T(8,128)(2,1)S(1)} %pad_maximum_fusion.2), channel_id=1, source_target_pairs={{0,32},{4,36},{8,40},{12,44},{16,48},{20,52},{24,56},{28,60},{32,6... | collective-permute-start | bytes 393224 | tf_op jit(solution)/shard_map/ppermute | solution.py:16
  451.5 20.7 %collective-permute-start.1 = (bf16[2,128,256]{2,1,0:T(8,128)(2,1)S(1)}, bf16[2,128,256]{2,1,0:T(8,128)(2,1)S(1)}, u32[]{:S(2)}, u32[]{:S(2)}) collective-permute-start(bf16[2,128,256]{2,1,0:T(8,128)(2,1)S(1)} %pad_maximum_fusion.2), channel_id=1, source_target_pairs={{0,28},{4,32},{8,36},{12,40},{16,44},{20,48},{24,52},{28,56},{32,6... | collective-permute-start | bytes 393224 | tf_op jit(solution)/shard_map/ppermute | solution.py:16
  456.8 18.7 %collective-permute-start.2 = (bf16[2,128,256]{2,1,0:T(8,128)(2,1)S(1)}, bf16[2,128,256]{2,1,0:T(8,128)(2,1)S(1)}, u32[]{:S(2)}, u32[]{:S(2)}) collective-permute-start(bf16[2,128,256]{2,1,0:T(8,128)(2,1)S(1)} %pad_maximum_fusion.2), channel_id=1, source_target_pairs={{0,24},{4,28},{8,32},{12,36},{16,40},{20,44},{24,48},{28,52},{32,5... | collective-permute-start | bytes 393224 | tf_op jit(solution)/shard_map/ppermute | solution.py:16
  460.9 16.8 %collective-permute-start.3 = (bf16[2,128,256]{2,1,0:T(8,128)(2,1)S(1)}, bf16[2,128,256]{2,1,0:T(8,128)(2,1)S(1)}, u32[]{:S(2)}, u32[]{:S(2)}) collective-permute-start(bf16[2,128,256]{2,1,0:T(8,128)(2,1)S(1)} %pad_maximum_fusion.2), channel_id=1, source_target_pairs={{0,20},{4,24},{8,28},{12,32},{16,36},{20,40},{24,44},{28,48},{32,5... | collective-permute-start | bytes 393224 | tf_op jit(solution)/shard_map/ppermute | solution.py:16
  463.8 14.0 %collective-permute-start.4 = (bf16[2,128,256]{2,1,0:T(8,128)(2,1)S(1)}, bf16[2,128,256]{2,1,0:T(8,128)(2,1)S(1)}, u32[]{:S(2)}, u32[]{:S(2)}) collective-permute-start(bf16[2,128,256]{2,1,0:T(8,128)(2,1)S(1)} %pad_maximum_fusion.2), channel_id=1, source_target_pairs={{0,16},{4,20},{8,24},{12,28},{16,32},{20,36},{24,40},{28,44},{32,4... | collective-permute-start | bytes 393224 | tf_op jit(solution)/shard_map/ppermute | solution.py:16
  468.2 9.6 collective-permute-start.5
  472.2 9.4 collective-permute-start.6
  475.6 9.0 collective-permute-start.7
  703.3 19.1 %collective-permute-start.15 = (f32[2,128,256]{1,2,0:T(8,128)}, f32[2,128,256]{1,2,0:T(8,128)}, u32[]{:S(2)}, u32[]{:S(2)}) collective-permute-start(f32[2,128,256]{1,2,0:T(8,128)} %get-tuple-element.8), channel_id=1, source_target_pairs={{32,0},{36,4},{40,8},{44,12},{48,16},{52,20},{56,24},{60,28},{64,3... | collective-permute-start | bytes 786440 | tf_op jit(solution)/shard_map/ppermute | solution.py:16
  704.5 21.3 %collective-permute-start.14 = (f32[2,128,256]{1,2,0:T(8,128)}, f32[2,128,256]{1,2,0:T(8,128)}, u32[]{:S(2)}, u32[]{:S(2)}) collective-permute-start(f32[2,128,256]{1,2,0:T(8,128)} %get-tuple-element.9), channel_id=1, source_target_pairs={{28,0},{32,4},{36,8},{40,12},{44,16},{48,20},{52,24},{56,28},{60,3... | collective-permute-start | bytes 786440 | tf_op jit(solution)/shard_map/ppermute | solution.py:16
  705.8 29.3 %collective-permute-start.13 = (f32[2,128,256]{1,2,0:T(8,128)}, f32[2,128,256]{1,2,0:T(8,128)}, u32[]{:S(2)}, u32[]{:S(2)}) collective-permute-start(f32[2,128,256]{1,2,0:T(8,128)} %get-tuple-element.7), channel_id=1, source_target_pairs={{24,0},{28,4},{32,8},{36,12},{40,16},{44,20},{48,24},{52,28},{56,3... | collective-permute-start | bytes 786440 | tf_op jit(solution)/shard_map/ppermute | solution.py:16
  707.1 39.9 %collective-permute-start.12 = (f32[2,128,256]{1,2,0:T(8,128)}, f32[2,128,256]{1,2,0:T(8,128)}, u32[]{:S(2)}, u32[]{:S(2)}) collective-permute-start(f32[2,128,256]{1,2,0:T(8,128)} %get-tuple-element.6), channel_id=1, source_target_pairs={{20,0},{24,4},{28,8},{32,12},{36,16},{40,20},{44,24},{48,28},{52,3... | collective-permute-start | bytes 786440 | tf_op jit(solution)/shard_map/ppermute | solution.py:16
  708.4 45.9 %collective-permute-start.11 = (f32[2,128,256]{1,2,0:T(8,128)}, f32[2,128,256]{1,2,0:T(8,128)}, u32[]{:S(2)}, u32[]{:S(2)}) collective-permute-start(f32[2,128,256]{1,2,0:T(8,128)} %get-tuple-element.5), channel_id=1, source_target_pairs={{16,0},{20,4},{24,8},{28,12},{32,16},{36,20},{40,24},{44,28},{48,3... | collective-permute-start | bytes 786440 | tf_op jit(solution)/shard_map/ppermute | solution.py:16
  722.3 32.1 %collective-permute-start.10 = (f32[2,128,256]{1,2,0:T(8,128)}, f32[2,128,256]{1,2,0:T(8,128)S(1)}, u32[]{:S(2)}, u32[]{:S(2)}) collective-permute-start(f32[2,128,256]{1,2,0:T(8,128)} %get-tuple-element.4), channel_id=1, source_target_pairs={{12,0},{16,4},{20,8},{24,12},{28,16},{32,20},{36,24},{40,28},{44,3... | collective-permute-start | bytes 786440 | tf_op jit(solution)/shard_map/ppermute | solution.py:16
  725.8 28.5 %collective-permute-start.9 = (f32[2,128,256]{1,2,0:T(8,128)}, f32[2,128,256]{1,2,0:T(8,128)S(1)}, u32[]{:S(2)}, u32[]{:S(2)}) collective-permute-start(f32[2,128,256]{1,2,0:T(8,128)} %get-tuple-element.3), channel_id=1, source_target_pairs={{8,0},{12,4},{16,8},{20,12},{24,16},{28,20},{32,24},{36,28},{40,32... | collective-permute-start | bytes 786440 | tf_op jit(solution)/shard_map/ppermute | solution.py:16
  735.2 19.2 %collective-permute-start.8 = (f32[2,128,256]{1,2,0:T(8,128)}, f32[2,128,256]{1,2,0:T(8,128)S(1)}, u32[]{:S(2)}, u32[]{:S(2)}) collective-permute-start(f32[2,128,256]{1,2,0:T(8,128)} %get-tuple-element.2), channel_id=1, source_target_pairs={{4,0},{8,4},{12,8},{16,12},{20,16},{24,20},{28,24},{32,28},{36,32}... | collective-permute-start | bytes 786440 | tf_op jit(solution)/shard_map/ppermute | solution.py:16
  744.9 9.5 copy-start.9
  744.9 9.5 copy-start.12
  759.8 8.9 copy-start.2
  759.8 8.9 copy-start.10
  1134.4 36.7 %collective-permute-start.31 = (f32[21,256]{1,0:T(8,128)S(1)}, f32[21,256]{1,0:T(8,128)S(1)}, u32[]{:S(2)}, u32[]{:S(2)}) collective-permute-start(f32[21,256]{1,0:T(8,128)S(1)} %slice.92), channel_id=1, source_target_pairs={{0,64},{4,68},{8,72},{12,76},{16,80},{20,84},{24,88},{28,92},{32,9... | collective-permute-start | bytes 64520
  1135.7 36.7 %collective-permute-start.30 = (f32[24,256]{1,0:T(8,128)S(1)}, f32[24,256]{1,0:T(8,128)S(1)}, u32[]{:S(2)}, u32[]{:S(2)}) collective-permute-start(f32[24,256]{1,0:T(8,128)S(1)} %fusion), channel_id=1, source_target_pairs={{0,60},{4,64},{8,68},{12,72},{16,76},{20,80},{24,84},{28,88},{32,9... | collective-permute-start | bytes 73736
  1137.0 51.5 %collective-permute-start.29 = (f32[24,256]{1,0:T(8,128)S(1)}, f32[24,256]{1,0:T(8,128)S(1)}, u32[]{:S(2)}, u32[]{:S(2)}) collective-permute-start(f32[24,256]{1,0:T(8,128)S(1)} %fusion), channel_id=1, source_target_pairs={{0,56},{4,60},{8,64},{12,68},{16,72},{20,76},{24,80},{28,84},{32,8... | collective-permute-start | bytes 73736
  1138.3 52.2 %collective-permute-start.28 = (f32[24,256]{1,0:T(8,128)S(1)}, f32[24,256]{1,0:T(8,128)S(1)}, u32[]{:S(2)}, u32[]{:S(2)}) collective-permute-start(f32[24,256]{1,0:T(8,128)S(1)} %fusion), channel_id=1, source_target_pairs={{0,52},{4,56},{8,60},{12,64},{16,68},{20,72},{24,76},{28,80},{32,8... | collective-permute-start | bytes 73736
  1169.7 23.2 %collective-permute-start.27 = (f32[24,256]{1,0:T(8,128)S(1)}, f32[24,256]{1,0:T(8,128)S(1)}, u32[]{:S(2)}, u32[]{:S(2)}) collective-permute-start(f32[24,256]{1,0:T(8,128)S(1)} %fusion), channel_id=1, source_target_pairs={{0,48},{4,52},{8,56},{12,60},{16,64},{20,68},{24,72},{28,76},{32,8... | collective-permute-start | bytes 73736
  1171.1 25.0 %collective-permute-start.26 = (f32[24,256]{1,0:T(8,128)S(1)}, f32[24,256]{1,0:T(8,128)S(1)}, u32[]{:S(2)}, u32[]{:S(2)}) collective-permute-start(f32[24,256]{1,0:T(8,128)S(1)} %fusion), channel_id=1, source_target_pairs={{0,44},{4,48},{8,52},{12,56},{16,60},{20,64},{24,68},{28,72},{32,7... | collective-permute-start | bytes 73736
  1172.4 25.9 %collective-permute-start.25 = (f32[24,256]{1,0:T(8,128)S(1)}, f32[24,256]{1,0:T(8,128)S(1)}, u32[]{:S(2)}, u32[]{:S(2)}) collective-permute-start(f32[24,256]{1,0:T(8,128)S(1)} %fusion), channel_id=1, source_target_pairs={{0,40},{4,44},{8,48},{12,52},{16,56},{20,60},{24,64},{28,68},{32,7... | collective-permute-start | bytes 73736
  1188.5 12.3 %collective-permute-start.24 = (f32[24,256]{1,0:T(8,128)S(1)}, f32[24,256]{1,0:T(8,128)S(1)}, u32[]{:S(2)}, u32[]{:S(2)}) collective-permute-start(f32[24,256]{1,0:T(8,128)S(1)} %fusion), channel_id=1, source_target_pairs={{0,36},{4,40},{8,44},{12,48},{16,52},{20,56},{24,60},{28,64},{32,6... | collective-permute-start | bytes 73736
  1190.4 14.6 %collective-permute-start.23 = (f32[24,256]{1,0:T(8,128)S(1)}, f32[24,256]{1,0:T(8,128)S(1)}, u32[]{:S(2)}, u32[]{:S(2)}) collective-permute-start(f32[24,256]{1,0:T(8,128)S(1)} %fusion), channel_id=1, source_target_pairs={{0,32},{4,36},{8,40},{12,44},{16,48},{20,52},{24,56},{28,60},{32,6... | collective-permute-start | bytes 73736
  1193.0 14.1 %collective-permute-start.22 = (f32[24,256]{1,0:T(8,128)S(1)}, f32[24,256]{1,0:T(8,128)S(1)}, u32[]{:S(2)}, u32[]{:S(2)}) collective-permute-start(f32[24,256]{1,0:T(8,128)S(1)} %fusion), channel_id=1, source_target_pairs={{0,28},{4,32},{8,36},{12,40},{16,44},{20,48},{24,52},{28,56},{32,6... | collective-permute-start | bytes 73736
  1196.0 14.9 %collective-permute-start.21 = (f32[24,256]{1,0:T(8,128)S(1)}, f32[24,256]{1,0:T(8,128)S(1)}, u32[]{:S(2)}, u32[]{:S(2)}) collective-permute-start(f32[24,256]{1,0:T(8,128)S(1)} %fusion), channel_id=1, source_target_pairs={{0,24},{4,28},{8,32},{12,36},{16,40},{20,44},{24,48},{28,52},{32,5... | collective-permute-start | bytes 73736
  1198.3 16.6 %collective-permute-start.20 = (f32[24,256]{1,0:T(8,128)S(1)}, f32[24,256]{1,0:T(8,128)S(1)}, u32[]{:S(2)}, u32[]{:S(2)}) collective-permute-start(f32[24,256]{1,0:T(8,128)S(1)} %fusion), channel_id=1, source_target_pairs={{0,20},{4,24},{8,28},{12,32},{16,36},{20,40},{24,44},{28,48},{32,5... | collective-permute-start | bytes 73736
  1200.8 14.0 %collective-permute-start.19 = (f32[24,256]{1,0:T(8,128)S(1)}, f32[24,256]{1,0:T(8,128)S(1)}, u32[]{:S(2)}, u32[]{:S(2)}) collective-permute-start(f32[24,256]{1,0:T(8,128)S(1)} %fusion), channel_id=1, source_target_pairs={{0,16},{4,20},{8,24},{12,28},{16,32},{20,36},{24,40},{28,44},{32,4... | collective-permute-start | bytes 73736
  1205.1 9.8 collective-permute-start.18
  1207.0 8.1 collective-permute-start.17
  1211.0 7.8 collective-permute-start.16
  (18 other events, 40.7 us)
Sparse Core Ops, SparseCore 0:
  12.3 234.7 all-gather.8
  251.3 192.8 all-gather.10
  448.8 214.4 all-gather.6
  771.9 36.5 reduce-scatter.3
